TPU v7x, 128 devices: a whole 4x4x4 slice. The times are simulated.
128 devices in a mesh: blk: 16 (over x, z), beam: 8 (over y, core).
Axes of the slice: x: 4, y: 4, z: 4, core: 2. Of those that a mesh axis runs over, the one named last changes fastest.
Arguments:
- embeds: bfloat16 [4, 128, 2048], P(None, 'beam'), may hold values from -6 to 6
- attn_gain: float32 [2048], replicated, may hold values from 0.25 to 1.75
- w_query: bfloat16 [2048, 3072], P(None, 'blk'), may hold values from -0.125 to 0.125
- w_latent: bfloat16 [2048, 576], replicated, may hold values from -0.125 to 0.125
- latent_gain: float32 [512], replicated, may hold values from 0.3 to 3
- w_key_up: bfloat16 [16, 128, 512], P('blk'), may hold values from -0.5 to 0.5
- w_value_up: bfloat16 [16, 512, 128], P('blk'), may hold values from -0.25 to 0.25
- w_out: bfloat16 [2048, 2048], P('blk'), may hold values from -0.125 to 0.125
- ffn_gain: float32 [2048], replicated, may hold values from 0.25 to 1.75
- w_shared_gate: bfloat16 [2048, 2816], P(None, 'blk'), may hold values from -0.125 to 0.125
- w_shared_up: bfloat16 [2048, 2816], P(None, 'blk'), may hold values from -0.125 to 0.125
- w_shared_down: bfloat16 [2816, 2048], P('blk'), may hold values from -0.109375 to 0.109375
- w_expert_gate: bfloat16 [32, 2048, 2816], P('blk', None, 'beam'), may hold values from -0.125 to 0.125
- w_expert_up: bfloat16 [32, 2048, 2816], P('blk', None, 'beam'), may hold values from -0.125 to 0.125
- w_expert_down: bfloat16 [32, 2816, 2048], P('blk', 'beam'), may hold values from -0.15625 to 0.15625
- cache_pool: bfloat16 [16, 96, 128, 576], P('beam', 'blk'), may hold values from -1600 to 1600
- block_tables: int32 [16, 8, 64], P('beam'), may hold values from 0 to 95, as said below
- block_counts: int32 [16], P('beam'), may hold values from 4 to 64
- parents: int32 [4, 16, 8], P(None, 'beam'), may hold values from 0 to 7
- expert_ids: int32 [4, 128, 6], replicated, may hold values from 0 to 63, all different within a row; in each aligned block of 128 rows (0 to 127, 128 to 255, ..., all dimensions but the last counted through in order) at most 24 rows name the same one
- expert_weights: float32 [4, 128, 6], replicated, may hold values from 0.1 to 0.6
Outputs:
- layer_out: float32 [4, 128, 2048], P(None, ('blk', 'beam'))
Inputs may be any that keep to these rules, and one draw needn't show every extreme that they name: `block_tables`: for each group g, entries j below block_counts[g] of one beam name different physical blocks; entries at or beyond block_counts[g] are never read. `expert_ids`: the experts of one row differ; within one step all rows together name one expert at most 24 times.
All inputs are finite; a program needn't handle non-finite values.
Results may differ from a plain program's by a relative error of at most 0.034.
Values may be sent and summed in bfloat16 or wider, within the bound.
No kernel may reach another device: no remote copies, remote signals or barrier semaphores. Data moves between devices by JAX's collectives and lax.ppermute only.
A program may use at most 128 MiB of HBM per device.

v0:
```python
import jax
import jax.numpy as jnp
from jax import lax
from jax.sharding import PartitionSpec as P

EXPERTS = 64
FFE = 1408
THETA = 50000.0
EPS = 1e-06
NEG = -1e30


def combined_all(shard, axis, combine):
    everything = jax.tree.map(lambda part: lax.all_gather(part, axis), shard)
    initial = jax.tree.map(lambda part: part[0], everything)

    def step(k, so_far):
        return combine(so_far, jax.tree.map(lambda part: part[k], everything))

    return lax.fori_loop(1, lax.axis_size(axis), step, initial)


def rms_scale(values, gain):
    mean_sq = jnp.mean(values * values, axis=-1, keepdims=True)
    return values * lax.rsqrt(mean_sq + EPS) * gain


def rotate(values, position):
    half_dim = values.shape[-1] // 2
    frequency = THETA ** (-jnp.arange(half_dim, dtype=jnp.float32) * 2.0 / values.shape[-1])
    angles = position[..., None] * frequency
    cosine = jnp.cos(angles)
    sine_part = jnp.sin(angles)
    lower_half = values[..., :half_dim]
    upper_half = values[..., half_dim:]
    return jnp.concatenate(
        [
            lower_half * cosine - upper_half * sine_part,
            lower_half * sine_part + upper_half * cosine,
        ],
        axis=-1,
    )


def combine(earlier, later):
    top_first, sum_first, lat_first = earlier
    top_second, sum_second, lat_second = later
    top_score = jnp.maximum(top_first, top_second)
    scale_first = jnp.exp(top_first - top_score)
    scale_second = jnp.exp(top_second - top_score)
    return (
        top_score,
        sum_first * scale_first + sum_second * scale_second,
        lat_first * scale_first[..., None] + lat_second * scale_second[..., None],
    )


def partial_attend(scores, key_mask, values, form):
    masked = jnp.where(key_mask, scores, NEG)
    top_score = jnp.max(masked, axis=-1)
    weights = jnp.where(key_mask, jnp.exp(masked - top_score[..., None]), 0.0)
    weight_sum = jnp.sum(weights, axis=-1)
    latent_sum = jnp.einsum(
        form, weights.astype(jnp.bfloat16), values, preferred_element_type=jnp.float32
    )
    return (top_score, weight_sum, latent_sum)


def per_device(
    embeds,
    attn_gain,
    w_query,
    w_latent,
    latent_gain,
    w_key_up,
    w_value_up,
    w_out,
    ffn_gain,
    w_shared_gate,
    w_shared_up,
    w_shared_down,
    w_expert_gate,
    w_expert_up,
    w_expert_down,
    cache_pool,
    block_tables,
    block_counts,
    parents,
    expert_ids,
    expert_weights,
):
    step_count, row_dev, model_width = embeds.shape
    group_count, beam_count, max_blocks = block_tables.shape
    heads_dev, head_in, latent = w_key_up.shape
    entry_width = cache_pool.shape[3]
    pool_dev = cache_pool.shape[1]
    block_len = cache_pool.shape[2]
    value_dim = w_value_up.shape[2]
    pair_dev = w_expert_gate.shape[0]
    unit_dev = w_expert_gate.shape[2]
    topk_count = expert_ids.shape[2]
    blk_index = lax.axis_index("blk")
    beam_index = lax.axis_index("beam")
    total_rows = row_dev * lax.axis_size("beam")
    capacity = 2 * total_rows * topk_count // EXPERTS
    score_scale = (entry_width - latent + head_in) ** (-0.5)
    phys_ids = blk_index * pool_dev + jnp.arange(pool_dev, dtype=jnp.int32)
    cache_keys = cache_pool.reshape(group_count, pool_dev * block_len, entry_width)
    cache_values = cache_keys[:, :, :latent]
    recent = jnp.zeros((group_count, beam_count, step_count, entry_width), jnp.bfloat16)
    tables = block_tables
    base_pos = (block_counts * block_len).astype(jnp.float32)
    valid = jnp.arange(max_blocks, dtype=jnp.int32)[None, None, :] < block_counts[:, None, None]
    pair_half = beam_index * unit_dev // FFE
    local_experts = (blk_index * pair_dev + jnp.arange(pair_dev, dtype=jnp.int32)) * 2 + pair_half
    results = []
    for decode_step in range(step_count):
        parent = parents[decode_step]
        recent = jnp.take_along_axis(recent, parent[:, :, None, None], axis=1)
        tables = jnp.take_along_axis(tables, parent[:, :, None], axis=1)
        tokens = embeds[decode_step]
        normed = rms_scale(tokens.astype(jnp.float32), attn_gain).astype(jnp.bfloat16)
        queries = jnp.dot(normed, w_query, preferred_element_type=jnp.float32).astype(jnp.bfloat16)
        queries = queries.reshape(row_dev, heads_dev, w_query.shape[1] // heads_dev)
        position = jnp.repeat(base_pos + decode_step, beam_count)
        query_latent = jnp.einsum(
            "rhn,hnc->rhc", queries[:, :, :head_in], w_key_up, preferred_element_type=jnp.float32
        )
        query_rope = rotate(queries[:, :, head_in:].astype(jnp.float32), position[:, None])
        query_full = jnp.concatenate([query_latent, query_rope], axis=-1).astype(jnp.bfloat16)
        projected = jnp.dot(normed, w_latent, preferred_element_type=jnp.float32)
        new_entry = jnp.concatenate(
            [
                rms_scale(projected[:, :latent], latent_gain),
                rotate(projected[:, latent:], position),
            ],
            axis=-1,
        ).astype(jnp.bfloat16)
        recent = recent.at[:, :, decode_step].set(
            new_entry.reshape(group_count, beam_count, entry_width)
        )
        all_queries = lax.all_gather(query_full, "blk", axis=1, tiled=True)
        head_count = all_queries.shape[1]
        grouped = all_queries.reshape(group_count, beam_count * head_count, entry_width)
        scores = (
            jnp.einsum("gqe,gke->gqk", grouped, cache_keys, preferred_element_type=jnp.float32)
            * score_scale
        )
        block_used = (
            jnp.sum(
                ((tables[:, :, :, None] == phys_ids) & valid[..., None]).astype(jnp.int32), axis=2
            )
            > 0
        )
        key_mask = jnp.repeat(jnp.repeat(block_used, block_len, axis=2), head_count, axis=1)
        top_score, weight_sum, latent_sum = partial_attend(
            scores, key_mask, cache_values, "gqk,gkc->gqc"
        )
        top_score = top_score.reshape(row_dev, head_count)
        weight_sum = weight_sum.reshape(row_dev, head_count)
        latent_sum = latent_sum.reshape(row_dev, head_count, latent)
        merged = combined_all((top_score, weight_sum, latent_sum), "blk", combine)
        head_start = blk_index * heads_dev
        pooled = tuple(
            (lax.dynamic_slice_in_dim(member, head_start, heads_dev, 1) for member in merged)
        )
        recent_rows = recent.reshape(row_dev, step_count, entry_width)[:, : decode_step + 1]
        recent_scores = (
            jnp.einsum("rhe,rse->rhs", query_full, recent_rows, preferred_element_type=jnp.float32)
            * score_scale
        )
        recent_part = partial_attend(
            recent_scores,
            jnp.ones(recent_scores.shape, bool),
            recent_rows[:, :, :latent],
            "rhs,rsc->rhc",
        )
        top_score, weight_sum, latent_sum = combine(pooled, recent_part)
        attended = (latent_sum / weight_sum[..., None]).astype(jnp.bfloat16)
        head_out = jnp.einsum(
            "rhc,hcv->rhv", attended, w_value_up, preferred_element_type=jnp.float32
        ).astype(jnp.bfloat16)
        attn_part = jnp.dot(
            head_out.reshape(row_dev, heads_dev * value_dim),
            w_out,
            preferred_element_type=jnp.float32,
        )
        attn_total = lax.psum(attn_part, "blk")
        resid = tokens.astype(jnp.float32) + attn_total
        ffn_in = rms_scale(resid, ffn_gain).astype(jnp.bfloat16)
        all_rows = lax.all_gather(ffn_in, "beam", axis=0, tiled=True)
        matches = expert_ids[decode_step][:, :, None] == local_experts
        routed = jnp.any(matches, axis=1)
        row_weight = jnp.sum(
            jnp.where(matches, expert_weights[decode_step][:, :, None], 0.0), axis=1
        )
        slot_index = jnp.cumsum(routed.astype(jnp.int32), axis=0) - 1
        slot_index = jnp.where(routed, slot_index, capacity)
        expert_cols = jnp.broadcast_to(
            jnp.arange(pair_dev, dtype=jnp.int32)[None, :], (total_rows, pair_dev)
        )
        row_numbers = jnp.broadcast_to(
            jnp.arange(total_rows, dtype=jnp.int32)[:, None], (total_rows, pair_dev)
        )
        slot_rows = (
            jnp.full((pair_dev, capacity), total_rows, jnp.int32)
            .at[expert_cols, slot_index]
            .set(row_numbers, mode="drop")
        )
        weight_pad = jnp.concatenate([row_weight.T, jnp.zeros((pair_dev, 1), jnp.float32)], axis=1)
        slot_weight = jnp.take_along_axis(weight_pad, slot_rows, axis=1)
        picked = jnp.take(all_rows, slot_rows, axis=0, mode="fill", fill_value=0)
        gate_val = jnp.einsum(
            "ecd,edf->ecf", picked, w_expert_gate, preferred_element_type=jnp.float32
        )
        up_val = jnp.einsum("ecd,edf->ecf", picked, w_expert_up, preferred_element_type=jnp.float32)
        activation = (jax.nn.silu(gate_val) * up_val).astype(jnp.bfloat16)
        down_out = (
            jnp.einsum(
                "ecf,efd->ecd", activation, w_expert_down, preferred_element_type=jnp.float32
            )
            * slot_weight[..., None]
        )
        partial_term = (
            jnp.zeros((total_rows, model_width), jnp.float32)
            .at[slot_rows.reshape(-1)]
            .add(down_out.reshape(-1, model_width), mode="drop")
        )
        shared_act = (
            jax.nn.silu(jnp.dot(ffn_in, w_shared_gate, preferred_element_type=jnp.float32))
            * jnp.dot(ffn_in, w_shared_up, preferred_element_type=jnp.float32)
        ).astype(jnp.bfloat16)
        own_rows = jnp.dot(
            shared_act, w_shared_down, preferred_element_type=jnp.float32
        ) + jnp.where(blk_index == 0, resid, 0.0)
        row_start = beam_index * row_dev
        partial_term = lax.dynamic_update_slice_in_dim(
            partial_term,
            lax.dynamic_slice_in_dim(partial_term, row_start, row_dev, 0) + own_rows,
            row_start,
            0,
        )
        summed = lax.psum_scatter(partial_term, ("blk", "beam"), scatter_dimension=0, tiled=True)
        results.append(summed)
    return jnp.stack(results)


def solution(mesh):
    placed = (
        P(None, "beam", None),
        P(),
        P(None, "blk"),
        P(),
        P(),
        P("blk", None, None),
        P("blk", None, None),
        P("blk", None),
        P(),
        P(None, "blk"),
        P(None, "blk"),
        P("blk", None),
        P("blk", None, "beam"),
        P("blk", None, "beam"),
        P("blk", "beam", None),
        P("beam", "blk", None, None),
        P("beam", None, None),
        P("beam"),
        P(None, "beam", None),
        P(),
        P(),
    )
    return jax.shard_map(
        per_device,
        mesh=mesh,
        in_specs=placed,
        out_specs=P(None, ("blk", "beam"), None),
        check_vma=False,
    )
```

profile of v0, /device:TPU:1, one launch (start us, length us, event | category | flops | bytes accessed | tf_op | source)
XLA Modules:
  0.0 969.4 jit_solution(11336190134766764950)
XLA Ops:
  19.6 20.8 %all_gather.60 = bf16[16,16,576]{2,0,1:T(8,128)(2,1)S(1)} all-gather(bf16[16,1,576]{2,0,1:T(8,128)(2,1)S(1)} %pad_maximum_fusion.4), channel_id=1, replica_groups=mesh['blk'=16,'beam'=8] {'blk'}, dimensions={1}, use_global_device_ids=true | all-gather | bytes 313344 | tf_op jit(solution)/shard_map/all_gather | solution.py:142
  55.1 18.1 %all_gather.65 = bf16[16,16,576]{2,0,1:T(8,128)(2,1)S(1)} all-gather(bf16[16,1,576]{2,0,1:T(8,128)(2,1)S(1)} %pad_maximum_fusion.5), channel_id=1, replica_groups=mesh['blk'=16,'beam'=8] {'blk'}, dimensions={1}, use_global_device_ids=true | all-gather | bytes 313344 | tf_op jit(solution)/shard_map/all_gather | solution.py:142
  77.3 19.4 %all_gather.70 = bf16[16,16,576]{2,0,1:T(8,128)(2,1)S(1)} all-gather(bf16[16,1,576]{2,0,1:T(8,128)(2,1)S(1)} %pad_maximum_fusion.6), channel_id=1, replica_groups=mesh['blk'=16,'beam'=8] {'blk'}, dimensions={1}, use_global_device_ids=true | all-gather | bytes 313344 | tf_op jit(solution)/shard_map/all_gather | solution.py:142
  102.2 19.3 %all_gather.75 = bf16[16,16,576]{2,0,1:T(8,128)(2,1)S(1)} all-gather(bf16[16,1,576]{2,0,1:T(8,128)(2,1)S(1)} %pad_maximum_fusion.7), channel_id=1, replica_groups=mesh['blk'=16,'beam'=8] {'blk'}, dimensions={1}, use_global_device_ids=true | all-gather | bytes 313344 | tf_op jit(solution)/shard_map/all_gather | solution.py:142
  130.3 11.5 %scatter_fusion.3 = s32[2,24]{1,0:T(2,128)S(1)} fusion(s32[2,24]{1,0:T(2,128)S(1)} %broadcast.828.clone, s32[256]{0:T(256)S(1)} %reshape.1849, s32[256]{0:T(256)S(1)} %reshape.1809), kind=kCustom, calls=%fused_computation.22 | custom fusion | bytes 5120 | tf_op jit(solution)/shard_map/scatter | solution.py:208
  158.6 11.5 %scatter_fusion.2 = s32[2,24]{1,0:T(2,128)S(1)} fusion(s32[2,24]{1,0:T(2,128)S(1)} %broadcast.828.clone.1, s32[256]{0:T(256)S(1)} %reshape.1835, s32[256]{0:T(256)S(1)} %reshape.1809), kind=kCustom, calls=%fused_computation.20 | custom fusion | bytes 5120 | tf_op jit(solution)/shard_map/scatter | solution.py:208
  209.0 19.1 %all_gather.61 = f32[16,16,16]{2,1,0:T(8,128)S(1)} all-gather(f32[1,16,16]{2,1,0:T(8,128)S(1)} %all_gather_reshape.36), channel_id=1, replica_groups=mesh['blk'=16,'beam'=8] {'blk'}, dimensions={0}, use_global_device_ids=true | all-gather | bytes 17408 | tf_op jit(solution)/shard_map/all_gather | solution.py:14
  228.2 18.1 %all_gather.62 = f32[16,16,16]{2,1,0:T(8,128)S(1)} all-gather(f32[1,16,16]{2,1,0:T(8,128)S(1)} %all_gather_reshape.37), channel_id=1, replica_groups=mesh['blk'=16,'beam'=8] {'blk'}, dimensions={0}, use_global_device_ids=true | all-gather | bytes 17408 | tf_op jit(solution)/shard_map/all_gather | solution.py:14
  252.9 19.4 %all_gather.66 = f32[16,16,16]{2,1,0:T(8,128)S(1)} all-gather(f32[1,16,16]{2,1,0:T(8,128)S(1)} %all_gather_reshape.39), channel_id=1, replica_groups=mesh['blk'=16,'beam'=8] {'blk'}, dimensions={0}, use_global_device_ids=true | all-gather | bytes 17408 | tf_op jit(solution)/shard_map/all_gather | solution.py:14
  273.0 16.5 %all_gather.67 = f32[16,16,16]{2,1,0:T(8,128)S(1)} all-gather(f32[1,16,16]{2,1,0:T(8,128)S(1)} %all_gather_reshape.40), channel_id=1, replica_groups=mesh['blk'=16,'beam'=8] {'blk'}, dimensions={0}, use_global_device_ids=true | all-gather | bytes 17408 | tf_op jit(solution)/shard_map/all_gather | solution.py:14
  295.8 18.2 %all_gather.71 = f32[16,16,16]{2,1,0:T(8,128)S(1)} all-gather(f32[1,16,16]{2,1,0:T(8,128)S(1)} %all_gather_reshape.42), channel_id=1, replica_groups=mesh['blk'=16,'beam'=8] {'blk'}, dimensions={0}, use_global_device_ids=true | all-gather | bytes 17408 | tf_op jit(solution)/shard_map/all_gather | solution.py:14
  314.8 18.2 %all_gather.72 = f32[16,16,16]{2,1,0:T(8,128)S(1)} all-gather(f32[1,16,16]{2,1,0:T(8,128)S(1)} %all_gather_reshape.43), channel_id=1, replica_groups=mesh['blk'=16,'beam'=8] {'blk'}, dimensions={0}, use_global_device_ids=true | all-gather | bytes 17408 | tf_op jit(solution)/shard_map/all_gather | solution.py:14
  338.0 18.5 %all_gather.76 = f32[16,16,16]{2,1,0:T(8,128)S(1)} all-gather(f32[1,16,16]{2,1,0:T(8,128)} %all_gather_reshape.45), channel_id=1, replica_groups=mesh['blk'=16,'beam'=8] {'blk'}, dimensions={0}, use_global_device_ids=true | all-gather | bytes 17408 | tf_op jit(solution)/shard_map/all_gather | solution.py:14
  357.3 15.7 %all_gather.77 = f32[16,16,16]{2,1,0:T(8,128)S(1)} all-gather(f32[1,16,16]{2,1,0:T(8,128)S(1)} %all_gather_reshape.46), channel_id=1, replica_groups=mesh['blk'=16,'beam'=8] {'blk'}, dimensions={0}, use_global_device_ids=true | all-gather | bytes 17408 | tf_op jit(solution)/shard_map/all_gather | solution.py:14
  390.7 29.7 %while.80 = (s32[]{:T(128)}, f32[16,16]{1,0:T(8,128)S(1)}, f32[16,16]{1,0:T(8,128)S(1)}, f32[16,16,512]{2,1,0:T(8,128)S(1)}, f32[16,16,16]{2,1,0:T(8,128)}, /*in...) while((s32[]{:T(128)}, f32[16,16]{1,0:T(8,128)S(1)}, ...), condition=%wide.region_8.10_spmd, body=%wide.region_7.9_spmd.sunk | while | flops 394757 | bytes 1583255 | solution.py:20
  423.9 29.6 %while.81 = (s32[]{:T(128)}, f32[16,16]{1,0:T(8,128)S(1)}, f32[16,16]{1,0:T(8,128)S(1)}, f32[16,16,512]{2,1,0:T(8,128)S(1)}, f32[16,16,16]{2,1,0:T(8,128)}, /*in...) while((s32[]{:T(128)}, f32[16,16]{1,0:T(8,128)S(1)}, ...), condition=%wide.region_23.28_spmd, body=%wide.region_22.27_spmd.sunk | while | flops 394757 | bytes 1583255 | solution.py:20
  457.2 29.6 %while.82 = (s32[]{:T(128)}, f32[16,16]{1,0:T(8,128)S(1)}, f32[16,16]{1,0:T(8,128)S(1)}, f32[16,16,512]{2,1,0:T(8,128)S(1)}, f32[16,16,16]{2,1,0:T(8,128)}, /*in...) while((s32[]{:T(128)}, f32[16,16]{1,0:T(8,128)S(1)}, ...), condition=%wide.region_40.45_spmd, body=%wide.region_39.44_spmd.sunk | while | flops 394757 | bytes 1583255 | solution.py:20
  490.4 38.8 %while.83 = (s32[]{:T(128)}, f32[16,16]{1,0:T(8,128)S(1)}, f32[16,16]{1,0:T(8,128)}, f32[16,16,512]{2,1,0:T(8,128)S(1)}, f32[16,16,16]{2,1,0:T(8,128)}, /*index=...) while((s32[]{:T(128)}, f32[16,16]{1,0:T(8,128)S(1)}, ...), condition=%wide.region_57.62_spmd, body=%wide.region_56.61_spmd.sunk | while | flops 394757 | bytes 1583255 | solution.py:20
  544.6 134.9 %all-reduce.15.cloned.1.call-done = (f32[16,2048]{1,0:T(8,128)}, f32[16,2048]{1,0:T(8,128)}, f32[16,2048]{1,0:T(8,128)}, f32[16,2048]{1,0:T(8,128)}) async-done(((f32[16,2048]{1,0:T(8,128)}, f32[16,2048]{1,0:T(8,128)}, f32[16,2048]{1,0:T(8,128)}, f32[16,2048]{1,0:T(8,128)}), (f32[16,2048]{1,0:T(8,128)}, f32[16,2048]{1,0:T(8,128)}, f32[16,2048]{1,0:T(8,128)}, ...) | async-done | bytes 524304 | tf_op jit(solution)/shard_map/psum | solution.py:188
  682.2 16.4 %all_gather.79 = bf16[128,2048]{1,0:T(8,128)(2,1)} all-gather(bf16[16,2048]{1,0:T(8,128)(2,1)S(1)} %get-tuple-element.895), channel_id=1, replica_groups=mesh['blk'=16,'beam'=8] {'beam'}, dimensions={0}, use_global_device_ids=true | all-gather | bytes 589824 | tf_op jit(solution)/shard_map/all_gather | solution.py:191
  700.7 14.3 %all_gather.74 = bf16[128,2048]{1,0:T(8,128)(2,1)} all-gather(bf16[16,2048]{1,0:T(8,128)(2,1)S(1)} %get-tuple-element.894), channel_id=1, replica_groups=mesh['blk'=16,'beam'=8] {'beam'}, dimensions={0}, use_global_device_ids=true | all-gather | bytes 589824 | tf_op jit(solution)/shard_map/all_gather | solution.py:191
  715.9 14.3 %all_gather.69 = bf16[128,2048]{1,0:T(8,128)(2,1)} all-gather(bf16[16,2048]{1,0:T(8,128)(2,1)S(1)} %get-tuple-element.893), channel_id=1, replica_groups=mesh['blk'=16,'beam'=8] {'beam'}, dimensions={0}, use_global_device_ids=true | all-gather | bytes 589824 | tf_op jit(solution)/shard_map/all_gather | solution.py:191
  731.1 14.2 %all_gather.64 = bf16[128,2048]{1,0:T(8,128)(2,1)} all-gather(bf16[16,2048]{1,0:T(8,128)(2,1)S(1)} %get-tuple-element.892), channel_id=1, replica_groups=mesh['blk'=16,'beam'=8] {'beam'}, dimensions={0}, use_global_device_ids=true | all-gather | bytes 589824 | tf_op jit(solution)/shard_map/all_gather | solution.py:191
  804.8 153.5 %all-reduce.13.cloned.1.call-done = (f32[128,2048]{1,0:T(8,128)}, f32[128,2048]{1,0:T(8,128)}, f32[128,2048]{1,0:T(8,128)}, f32[128,2048]{1,0:T(8,128)}) async-done(((f32[128,2048]{1,0:T(8,128)}, f32[128,2048]{1,0:T(8,128)}, f32[128,2048]{1,0:T(8,128)}, f32[128,2048]{1,0:T(8,128)}), (f32[128,2048]{1,0:T(8,128)}, f32[128,2048]{1,0:T(8,128)}, f32[128,2048]{1,0:T(8,128)}, ...) | async-done | bytes 4194320
  (624 shorter events, 360.5 us)
Async XLA Ops:
  6.5 744.5 %copy-start = (bf16[2,352,2048]{2,1,0:T(8,128)(2,1)S(1)}, bf16[2,352,2048]{2,1,0:T(8,128)(2,1)}, u32[]{:S(2)}) copy-start(bf16[2,352,2048]{2,1,0:T(8,128)(2,1)} %param.59) | copy-start | bytes 8650756
  6.5 383.1 %all-gather.5.cloned.1.call-start = ((), (), s32[]{:S(2)}) async-start(), calls=%async_computation | async-start | bytes 8912896 | tf_op jit(solution)/shard_map/all_gather | solution.py:14
  49.0 373.9 %all-gather.7.cloned.1.call-start = ((), (), s32[]{:S(2)}) async-start(), calls=%async_computation.1 | async-start | bytes 8912896 | tf_op jit(solution)/shard_map/all_gather | solution.py:14
  76.5 379.6 %all-gather.9.cloned.1.call-start = ((), (), s32[]{:S(2)}) async-start(), calls=%async_computation.2 | async-start | bytes 8912896 | tf_op jit(solution)/shard_map/all_gather | solution.py:14
  101.4 387.8 %all-gather.11.cloned.1.call-start = ((), (), s32[]{:S(2)}) async-start(), calls=%async_computation.3 | async-start | bytes 8912896 | tf_op jit(solution)/shard_map/all_gather | solution.py:14
  126.3 553.2 %all-reduce.15.cloned.1.call-start = ((), (), s32[]{:S(2)}) async-start(), calls=%async_computation.5 | async-start | bytes 1048576 | tf_op jit(solution)/shard_map/psum | solution.py:188
  192.1 58.9 %copy-start.35 = (bf16[16,512]{1,0:T(8,128)(2,1)S(1)}, bf16[16,512]{1,0:T(8,128)(2,1)}, u32[]{:S(2)}) copy-start(bf16[16,512]{1,0:T(8,128)(2,1)} %copy-done.34) | copy-start | bytes 49156
  192.1 58.9 %copy-start.58 = (bf16[16,1,32]{2,0,1:T(8,128)(2,1)S(1)}, bf16[16,1,32]{2,0,1:T(8,128)(2,1)}, u32[]{:S(2)}) copy-start(bf16[16,1,32]{2,0,1:T(8,128)(2,1)} %copy-done.57) | copy-start | bytes 3076
  192.1 58.9 %copy-start.60 = (bf16[16,1,32]{2,0,1:T(8,128)(2,1)S(1)}, bf16[16,1,32]{2,0,1:T(8,128)(2,1)}, u32[]{:S(2)}) copy-start(bf16[16,1,32]{2,0,1:T(8,128)(2,1)} %copy-done.59) | copy-start | bytes 3076
  203.6 90.4 %copy-start.33 = (bf16[16,512]{1,0:T(8,128)(2,1)S(1)}, bf16[16,512]{1,0:T(8,128)(2,1)}, u32[]{:S(2)}) copy-start(bf16[16,512]{1,0:T(8,128)(2,1)} %copy-done.32) | copy-start | bytes 49156
  203.6 90.4 %copy-start.54 = (bf16[16,1,32]{2,0,1:T(8,128)(2,1)S(1)}, bf16[16,1,32]{2,0,1:T(8,128)(2,1)}, u32[]{:S(2)}) copy-start(bf16[16,1,32]{2,0,1:T(8,128)(2,1)} %copy-done.53) | copy-start | bytes 3076
  203.6 90.4 %copy-start.56 = (bf16[16,1,32]{2,0,1:T(8,128)(2,1)S(1)}, bf16[16,1,32]{2,0,1:T(8,128)(2,1)}, u32[]{:S(2)}) copy-start(bf16[16,1,32]{2,0,1:T(8,128)(2,1)} %copy-done.55) | copy-start | bytes 3076
  203.6 132.3 %copy-start.31 = (bf16[16,512]{1,0:T(8,128)(2,1)S(1)}, bf16[16,512]{1,0:T(8,128)(2,1)}, u32[]{:S(2)}) copy-start(bf16[16,512]{1,0:T(8,128)(2,1)} %copy-done.30) | copy-start | bytes 49156
  203.6 132.3 %copy-start.50 = (bf16[16,1,32]{2,0,1:T(8,128)(2,1)S(1)}, bf16[16,1,32]{2,0,1:T(8,128)(2,1)}, u32[]{:S(2)}) copy-start(bf16[16,1,32]{2,0,1:T(8,128)(2,1)} %copy-done.49) | copy-start | bytes 3076
  203.6 132.3 %copy-start.52 = (bf16[16,1,32]{2,0,1:T(8,128)(2,1)S(1)}, bf16[16,1,32]{2,0,1:T(8,128)(2,1)}, u32[]{:S(2)}) copy-start(bf16[16,1,32]{2,0,1:T(8,128)(2,1)} %copy-done.51) | copy-start | bytes 3076
  273.0 111.9 %copy-start.81 = (s32[2,24]{1,0:T(2,128)S(1)}, s32[2,24]{1,0:T(2,128)}, u32[]{:S(2)}) copy-start(s32[2,24]{1,0:T(2,128)} %compare_select_fusion.13) | copy-start | bytes 580
  273.0 113.7 %copy-start.67 = (f32[128,2]{0,1:T(2,128)S(1)}, f32[128,2]{0,1:T(2,128)}, u32[]{:S(2)}) copy-start(f32[128,2]{0,1:T(2,128)} %get-tuple-element.793) | copy-start | bytes 3076
  295.0 94.0 %copy-start.82 = (s32[2,24]{1,0:T(2,128)S(1)}, s32[2,24]{1,0:T(2,128)}, u32[]{:S(2)}) copy-start(s32[2,24]{1,0:T(2,128)} %compare_select_fusion.15) | copy-start | bytes 580
  530.2 149.3 %copy-start.8 = (bf16[4,16,2048]{2,1,0:T(8,128)(2,1)S(1)}, bf16[4,16,2048]{2,1,0:T(8,128)(2,1)}, u32[]{:S(2)}) copy-start(bf16[4,16,2048]{2,1,0:T(8,128)(2,1)} %param.45) | copy-start | bytes 786436
  530.2 150.8 %copy-start.63 = (f32[2048]{0:T(1024)S(1)}, f32[2048]{0:T(1024)}, u32[]{:S(2)}) copy-start(f32[2048]{0:T(1024)} %param.53) | copy-start | bytes 24580
  542.2 416.1 %all-reduce.13.cloned.1.call-start = ((), (), s32[]{:S(2)}) async-start(), calls=%async_computation.4 | async-start | bytes 8388608
  682.2 63.1 %copy-start.15 = (bf16[16,2048]{1,0:T(8,128)(2,1)}, bf16[16,2048]{1,0:T(8,128)(2,1)S(1)}, u32[]{:S(2)}) copy-start(bf16[16,2048]{1,0:T(8,128)(2,1)S(1)} %get-tuple-element.893) | copy-start | bytes 196612
  682.2 63.1 %copy-start.16 = (bf16[16,2048]{1,0:T(8,128)(2,1)}, bf16[16,2048]{1,0:T(8,128)(2,1)S(1)}, u32[]{:S(2)}) copy-start(bf16[16,2048]{1,0:T(8,128)(2,1)S(1)} %get-tuple-element.894) | copy-start | bytes 196612
  682.2 63.1 %copy-start.18 = (bf16[16,2048]{1,0:T(8,128)(2,1)}, bf16[16,2048]{1,0:T(8,128)(2,1)S(1)}, u32[]{:S(2)}) copy-start(bf16[16,2048]{1,0:T(8,128)(2,1)S(1)} %get-tuple-element.895) | copy-start | bytes 196612
  (68 other events, 1006.1 us)
Sparse Core Ops, SparseCore 0:
  49.1 78.4 all-gather.4
  129.8 70.4 all-gather.6
  202.5 71.7 all-gather.8
  276.2 71.4 all-gather.10
  542.4 137.1 all-reduce.14
  804.9 153.3 all-reduce.12
where the time goes:
time: 984 us; the launch traced here: 969 us
  waiting for transfers between devices  288 us (29%)
  blocking collectives  281 us (29%)
  other arithmetic  187 us (19%)
  local copies, waits for them, and re-layouts  113 us (11%)
  matrix products  82.2 us (8%)
  between operations  15.3 us (2%)
    unnamed x7, waiting for transfers between devices  154 us
    all_gather x8, blocking collectives, combined_all(): everything = jax.tree.map(lambda part: lax.all_gather(part, axis), shard)  144 us
    psum x1, waiting for transfers between devices, per_device(): attn_total = lax.psum(attn_part, 'blk')  135 us
    all_gather x4, blocking collectives, per_device(): all_queries = lax.all_gather(query_full, 'blk', axis=1, tiled=True)  77.6 us
    add x60, other arithmetic, combine(): lat_first * scale_first[..., None] + lat_second * scale_second[..., None]  72.7 us
    all_gather x4, blocking collectives, per_device(): all_rows = lax.all_gather(ffn_in, 'beam', axis=0, tiled=True)  59.2 us
    add x60, other arithmetic, combine(): sum_first * scale_first + sum_second * scale_second  53.2 us
    scatter x4, local copies, waits for them, and re-layouts, per_device(): slot_rows = jnp.full((pair_dev, capacity), total_rows, jnp.int32).at[expe...  45.8 us
  transfers between devices with their start and end apart: 6, of which 2 were waited for; matrix products, arithmetic and copies ran while one was open for 24% of the time, Pallas kernels for 0%

commit v1 on v0

--- a/solution.py
+++ b/solution.py
@@ -8,6 +8,14 @@
 THETA = 50000.0
 EPS = 1e-06
 NEG = -1e30
+
+
+def add_in_pairs(x, mesh_axis):
+    n_dev, total = (lax.axis_size(mesh_axis), x)
+    for far in [1 << k for k in range(n_dev.bit_length() - 1)]:
+        swap = [(i, i ^ far) for i in range(n_dev)]
+        total = total + lax.ppermute(total, mesh_axis, swap)
+    return total
 
 
 def combined_all(shard, axis, combine):
@@ -185,7 +193,7 @@
             w_out,
             preferred_element_type=jnp.float32,
         )
-        attn_total = lax.psum(attn_part, "blk")
+        attn_total = add_in_pairs(attn_part, "blk")
         resid = tokens.astype(jnp.float32) + attn_total
         ffn_in = rms_scale(resid, ffn_gain).astype(jnp.bfloat16)
         all_rows = lax.all_gather(ffn_in, "beam", axis=0, tiled=True)

time: 984 us -> 937 us (0.952)
  waiting for transfers between devices: 288 us -> 156 us
  blocking collectives: 281 us -> 335 us
  other arithmetic: 187 us -> 207 us
  starting transfers between devices: 0.38 us -> 19.5 us
    psum x1 -> x0, waiting for transfers between devices: 135 us -> none  [per_device(): attn_total = lax.psum(attn_part, 'blk')]
    all_gather x4, blocking collectives: 59.2 us -> 113 us  [per_device(): all_rows = lax.all_gather(ffn_in, 'beam', axis=0, tiled=True)]
    add x60, other arithmetic: 53.2 us -> 72.4 us  [combine(): sum_first * scale_first + sum_second * scale_second]
    ppermute x0 -> x16, starting transfers between devices: none -> 19.2 us  [add_in_pairs(): total = total + lax.ppermute(total, mesh_axis, swap)]
    unnamed x7 -> x6, waiting for transfers between devices: 154 us -> 153 us
  transfers between devices with their start and end apart: 6 -> 21, of which waited for: 2 -> 2; matrix products, arithmetic and copies ran while one was open for 24% -> 32% of each run, Pallas kernels for 0% -> 0%
where the time goes in v1:
time: 937 us; the launch traced here: 923 us
  blocking collectives  335 us (36%)
  other arithmetic  207 us (22%)
  waiting for transfers between devices  156 us (17%)
  local copies, waits for them, and re-layouts  108 us (12%)
  matrix products  81.7 us (9%)
  starting transfers between devices  19.5 us (2%)
  between operations  15.3 us (2%)
    unnamed x6, waiting for transfers between devices  153 us
    all_gather x8, blocking collectives, combined_all(): everything = jax.tree.map(lambda part: lax.all_gather(part, axis), shard)  144 us
    all_gather x4, blocking collectives, per_device(): all_rows = lax.all_gather(ffn_in, 'beam', axis=0, tiled=True)  113 us
    all_gather x4, blocking collectives, per_device(): all_queries = lax.all_gather(query_full, 'blk', axis=1, tiled=True)  77.3 us
    add x60, other arithmetic, combine(): lat_first * scale_first[..., None] + lat_second * scale_second[..., None]  72.4 us
    add x60, other arithmetic, combine(): sum_first * scale_first + sum_second * scale_second  72.4 us
    scatter x4, local copies, waits for them, and re-layouts, per_device(): slot_rows = jnp.full((pair_dev, capacity), total_rows, jnp.int32).at[expe...  45.8 us
    ppermute x16, starting transfers between devices, add_in_pairs(): total = total + lax.ppermute(total, mesh_axis, swap)  19.2 us
  transfers between devices with their start and end apart: 21, of which 2 were waited for; matrix products, arithmetic and copies ran while one was open for 32% of the time, Pallas kernels for 0%

profile of v1, /device:TPU:1, one launch (start us, length us, event | category | flops | bytes accessed | tf_op | source)
XLA Modules:
  0.0 922.8 jit_solution(4268031375788828202)
XLA Ops:
  22.7 20.8 %all_gather.60 = bf16[16,16,576]{2,0,1:T(8,128)(2,1)S(1)} all-gather(bf16[16,1,576]{2,0,1:T(8,128)(2,1)S(1)} %pad_maximum_fusion.4), channel_id=1, replica_groups=mesh['blk'=16,'beam'=8] {'blk'}, dimensions={1}, use_global_device_ids=true | all-gather | bytes 313344 | tf_op jit(solution)/shard_map/all_gather | solution.py:150
  55.6 18.1 %all_gather.65 = bf16[16,16,576]{2,0,1:T(8,128)(2,1)S(1)} all-gather(bf16[16,1,576]{2,0,1:T(8,128)(2,1)S(1)} %pad_maximum_fusion.5), channel_id=1, replica_groups=mesh['blk'=16,'beam'=8] {'blk'}, dimensions={1}, use_global_device_ids=true | all-gather | bytes 313344 | tf_op jit(solution)/shard_map/all_gather | solution.py:150
  79.2 18.8 %all_gather.70 = bf16[16,16,576]{2,0,1:T(8,128)(2,1)S(1)} all-gather(bf16[16,1,576]{2,0,1:T(8,128)(2,1)S(1)} %pad_maximum_fusion.6), channel_id=1, replica_groups=mesh['blk'=16,'beam'=8] {'blk'}, dimensions={1}, use_global_device_ids=true | all-gather | bytes 313344 | tf_op jit(solution)/shard_map/all_gather | solution.py:150
  103.6 19.6 %all_gather.75 = bf16[16,16,576]{2,0,1:T(8,128)(2,1)S(1)} all-gather(bf16[16,1,576]{2,0,1:T(8,128)(2,1)S(1)} %pad_maximum_fusion.7), channel_id=1, replica_groups=mesh['blk'=16,'beam'=8] {'blk'}, dimensions={1}, use_global_device_ids=true | all-gather | bytes 313344 | tf_op jit(solution)/shard_map/all_gather | solution.py:150
  132.1 11.5 %scatter_fusion.3 = s32[2,24]{1,0:T(2,128)S(1)} fusion(s32[2,24]{1,0:T(2,128)S(1)} %broadcast.828.clone, s32[256]{0:T(256)S(1)} %reshape.1849, s32[256]{0:T(256)S(1)} %reshape.1809), kind=kCustom, calls=%fused_computation.22 | custom fusion | bytes 5120 | tf_op jit(solution)/shard_map/scatter | solution.py:216
  157.2 11.5 %scatter_fusion.2 = s32[2,24]{1,0:T(2,128)S(1)} fusion(s32[2,24]{1,0:T(2,128)S(1)} %broadcast.828.clone.1, s32[256]{0:T(256)S(1)} %reshape.1835, s32[256]{0:T(256)S(1)} %reshape.1809), kind=kCustom, calls=%fused_computation.20 | custom fusion | bytes 5120 | tf_op jit(solution)/shard_map/scatter | solution.py:216
  172.8 11.5 %scatter_fusion.1 = s32[2,24]{1,0:T(2,128)S(1)} fusion(s32[2,24]{1,0:T(2,128)S(1)} %broadcast.828.clone.2, s32[256]{0:T(256)S(1)} %reshape.1821, s32[256]{0:T(256)S(1)} %reshape.1809), kind=kCustom, calls=%fused_computation.18 | custom fusion | bytes 5120 | tf_op jit(solution)/shard_map/scatter | solution.py:216
  205.0 18.1 %all_gather.61 = f32[16,16,16]{2,1,0:T(8,128)S(1)} all-gather(f32[1,16,16]{2,1,0:T(8,128)S(1)} %all_gather_reshape.36), channel_id=1, replica_groups=mesh['blk'=16,'beam'=8] {'blk'}, dimensions={0}, use_global_device_ids=true | all-gather | bytes 17408 | tf_op jit(solution)/shard_map/all_gather | solution.py:22
  224.4 16.5 %all_gather.62 = f32[16,16,16]{2,1,0:T(8,128)S(1)} all-gather(f32[1,16,16]{2,1,0:T(8,128)S(1)} %all_gather_reshape.37), channel_id=1, replica_groups=mesh['blk'=16,'beam'=8] {'blk'}, dimensions={0}, use_global_device_ids=true | all-gather | bytes 17408 | tf_op jit(solution)/shard_map/all_gather | solution.py:22
  246.0 20.4 %all_gather.66 = f32[16,16,16]{2,1,0:T(8,128)S(1)} all-gather(f32[1,16,16]{2,1,0:T(8,128)S(1)} %all_gather_reshape.39), channel_id=1, replica_groups=mesh['blk'=16,'beam'=8] {'blk'}, dimensions={0}, use_global_device_ids=true | all-gather | bytes 17408 | tf_op jit(solution)/shard_map/all_gather | solution.py:22
  267.2 16.3 %all_gather.67 = f32[16,16,16]{2,1,0:T(8,128)S(1)} all-gather(f32[1,16,16]{2,1,0:T(8,128)S(1)} %all_gather_reshape.40), channel_id=1, replica_groups=mesh['blk'=16,'beam'=8] {'blk'}, dimensions={0}, use_global_device_ids=true | all-gather | bytes 17408 | tf_op jit(solution)/shard_map/all_gather | solution.py:22
  287.8 19.5 %all_gather.71 = f32[16,16,16]{2,1,0:T(8,128)S(1)} all-gather(f32[1,16,16]{2,1,0:T(8,128)S(1)} %all_gather_reshape.42), channel_id=1, replica_groups=mesh['blk'=16,'beam'=8] {'blk'}, dimensions={0}, use_global_device_ids=true | all-gather | bytes 17408 | tf_op jit(solution)/shard_map/all_gather | solution.py:22
  308.7 17.2 %all_gather.72 = f32[16,16,16]{2,1,0:T(8,128)S(1)} all-gather(f32[1,16,16]{2,1,0:T(8,128)S(1)} %all_gather_reshape.43), channel_id=1, replica_groups=mesh['blk'=16,'beam'=8] {'blk'}, dimensions={0}, use_global_device_ids=true | all-gather | bytes 17408 | tf_op jit(solution)/shard_map/all_gather | solution.py:22
  330.2 20.5 %all_gather.76 = f32[16,16,16]{2,1,0:T(8,128)S(1)} all-gather(f32[1,16,16]{2,1,0:T(8,128)S(1)} %all_gather_reshape.45), channel_id=1, replica_groups=mesh['blk'=16,'beam'=8] {'blk'}, dimensions={0}, use_global_device_ids=true | all-gather | bytes 17408 | tf_op jit(solution)/shard_map/all_gather | solution.py:22
  350.7 15.4 %all_gather.77 = f32[16,16,16]{2,1,0:T(8,128)S(1)} all-gather(f32[1,16,16]{2,1,0:T(8,128)S(1)} %all_gather_reshape.46), channel_id=1, replica_groups=mesh['blk'=16,'beam'=8] {'blk'}, dimensions={0}, use_global_device_ids=true | all-gather | bytes 17408 | tf_op jit(solution)/shard_map/all_gather | solution.py:22
  373.9 39.0 %while.80 = (s32[]{:T(128)}, f32[16,16]{1,0:T(8,128)}, f32[16,16]{1,0:T(8,128)}, f32[16,16,512]{2,1,0:T(8,128)S(1)}, f32[16,16,16]{2,1,0:T(8,128)}, /*index=5*/f...) while((s32[]{:T(128)}, f32[16,16]{1,0:T(8,128)}, ...), condition=%wide.region_8.10_spmd, body=%wide.region_7.9_spmd.sunk | while | flops 394757 | bytes 1583255 | solution.py:28
  421.3 38.9 %while.81 = (s32[]{:T(128)}, f32[16,16]{1,0:T(8,128)}, f32[16,16]{1,0:T(8,128)}, f32[16,16,512]{2,1,0:T(8,128)S(1)}, f32[16,16,16]{2,1,0:T(8,128)}, /*index=5*/f...) while((s32[]{:T(128)}, f32[16,16]{1,0:T(8,128)}, ...), condition=%wide.region_22.27_spmd, body=%wide.region_21.26_spmd.sunk | while | flops 394757 | bytes 1583255 | solution.py:28
  466.8 39.0 %while.82 = (s32[]{:T(128)}, f32[16,16]{1,0:T(8,128)}, f32[16,16]{1,0:T(8,128)}, f32[16,16,512]{2,1,0:T(8,128)S(1)}, f32[16,16,16]{2,1,0:T(8,128)}, /*index=5*/f...) while((s32[]{:T(128)}, f32[16,16]{1,0:T(8,128)}, ...), condition=%wide.region_38.43_spmd, body=%wide.region_37.42_spmd.sunk | while | flops 394757 | bytes 1583255 | solution.py:28
  513.8 29.6 %while.83 = (s32[]{:T(128)}, f32[16,16]{1,0:T(8,128)S(1)}, f32[16,16]{1,0:T(8,128)S(1)}, f32[16,16,512]{2,1,0:T(8,128)S(1)}, f32[16,16,16]{2,1,0:T(8,128)}, /*in...) while((s32[]{:T(128)}, f32[16,16]{1,0:T(8,128)S(1)}, ...), condition=%wide.region_54.59_spmd, body=%wide.region_53.58_spmd.sunk | while | flops 394757 | bytes 1583255 | solution.py:28
  581.8 71.8 %all_gather.79 = bf16[128,2048]{1,0:T(8,128)(2,1)} all-gather(bf16[16,2048]{1,0:T(8,128)(2,1)S(1)} %get-tuple-element.934), channel_id=1, replica_groups=mesh['blk'=16,'beam'=8] {'beam'}, dimensions={0}, use_global_device_ids=true | all-gather | bytes 589824 | tf_op jit(solution)/shard_map/all_gather | solution.py:199
  654.5 14.2 %all_gather.74 = bf16[128,2048]{1,0:T(8,128)(2,1)} all-gather(bf16[16,2048]{1,0:T(8,128)(2,1)S(1)} %get-tuple-element.933), channel_id=1, replica_groups=mesh['blk'=16,'beam'=8] {'beam'}, dimensions={0}, use_global_device_ids=true | all-gather | bytes 589824 | tf_op jit(solution)/shard_map/all_gather | solution.py:199
  669.6 14.2 %all_gather.69 = bf16[128,2048]{1,0:T(8,128)(2,1)} all-gather(bf16[16,2048]{1,0:T(8,128)(2,1)S(1)} %get-tuple-element.932), channel_id=1, replica_groups=mesh['blk'=16,'beam'=8] {'beam'}, dimensions={0}, use_global_device_ids=true | all-gather | bytes 589824 | tf_op jit(solution)/shard_map/all_gather | solution.py:199
  684.7 13.1 %all_gather.64 = bf16[128,2048]{1,0:T(8,128)(2,1)S(1)} all-gather(bf16[16,2048]{1,0:T(8,128)(2,1)S(1)} %get-tuple-element.931), channel_id=1, replica_groups=mesh['blk'=16,'beam'=8] {'beam'}, dimensions={0}, use_global_device_ids=true | all-gather | bytes 589824 | tf_op jit(solution)/shard_map/all_gather | solution.py:199
  759.1 152.6 %all-reduce.11.cloned.1.call-done = (f32[128,2048]{1,0:T(8,128)}, f32[128,2048]{1,0:T(8,128)}, f32[128,2048]{1,0:T(8,128)}, f32[128,2048]{1,0:T(8,128)}) async-done(((f32[128,2048]{1,0:T(8,128)}, f32[128,2048]{1,0:T(8,128)}, f32[128,2048]{1,0:T(8,128)}, f32[128,2048]{1,0:T(8,128)}), (f32[128,2048]{1,0:T(8,128)}, f32[128,2048]{1,0:T(8,128)}, f32[128,2048]{1,0:T(8,128)}, ...) | async-done | bytes 4194320
  (667 shorter events, 384.1 us)
Async XLA Ops:
  6.5 697.8 %copy-start = (bf16[2,352,2048]{2,1,0:T(8,128)(2,1)S(1)}, bf16[2,352,2048]{2,1,0:T(8,128)(2,1)}, u32[]{:S(2)}) copy-start(bf16[2,352,2048]{2,1,0:T(8,128)(2,1)} %param.59) | copy-start | bytes 8650756
  6.5 366.3 %all-gather.5.cloned.1.call-start = ((), (), s32[]{:S(2)}) async-start(), calls=%async_computation | async-start | bytes 8912896 | tf_op jit(solution)/shard_map/all_gather | solution.py:22
  53.0 367.3 %all-gather.7.cloned.1.call-start = ((), (), s32[]{:S(2)}) async-start(), calls=%async_computation.1 | async-start | bytes 8912896 | tf_op jit(solution)/shard_map/all_gather | solution.py:22
  78.4 387.3 %all-gather.9.cloned.1.call-start = ((), (), s32[]{:S(2)}) async-start(), calls=%async_computation.2 | async-start | bytes 8912896 | tf_op jit(solution)/shard_map/all_gather | solution.py:22
  102.8 409.9 %all-gather.11.cloned.1.call-start = ((), (), s32[]{:S(2)}) async-start(), calls=%async_computation.3 | async-start | bytes 8912896 | tf_op jit(solution)/shard_map/all_gather | solution.py:22
  128.0 783.7 %all-reduce.11.cloned.1.call-start = ((), (), s32[]{:S(2)}) async-start(), calls=%async_computation.4 | async-start | bytes 8388608
  200.6 127.5 %copy-start.35 = (bf16[16,512]{1,0:T(8,128)(2,1)S(1)}, bf16[16,512]{1,0:T(8,128)(2,1)}, u32[]{:S(2)}) copy-start(bf16[16,512]{1,0:T(8,128)(2,1)} %copy-done.34) | copy-start | bytes 49156
  203.3 147.3 %copy-start.70 = (f32[2,128]{1,0:T(2,128)S(1)}, f32[2,128]{1,0:T(2,128)}, u32[]{:S(2)}) copy-start(f32[2,128]{1,0:T(2,128)} %get-tuple-element.891) | copy-start | bytes 3076
  418.4 129.6 %collective-permute-start = (f32[16,2048]{1,0:T(8,128)}, f32[16,2048]{1,0:T(8,128)}, u32[]{:S(2)}, u32[]{:S(2)}) collective-permute-start(f32[16,2048]{1,0:T(8,128)} %fusion.32), channel_id=1, source_target_pairs={{0,8},{8,0},{16,24},{24,16},{32,40},{40,32},{48,56},{56,48},{64,72... | collective-permute-start | bytes 393224 | tf_op jit(solution)/shard_map/ppermute | solution.py:17
  465.7 85.4 %collective-permute-start.4 = (f32[16,2048]{1,0:T(8,128)}, f32[16,2048]{1,0:T(8,128)}, u32[]{:S(2)}, u32[]{:S(2)}) collective-permute-start(f32[16,2048]{1,0:T(8,128)} %fusion.33), channel_id=1, source_target_pairs={{0,8},{8,0},{16,24},{24,16},{32,40},{40,32},{48,56},{56,48},{64,72... | collective-permute-start | bytes 393224 | tf_op jit(solution)/shard_map/ppermute | solution.py:17
  511.3 41.8 %collective-permute-start.8 = (f32[16,2048]{1,0:T(8,128)}, f32[16,2048]{1,0:T(8,128)}, u32[]{:S(2)}, u32[]{:S(2)}) collective-permute-start(f32[16,2048]{1,0:T(8,128)} %fusion.34), channel_id=1, source_target_pairs={{0,8},{8,0},{16,24},{24,16},{32,40},{40,32},{48,56},{56,48},{64,72... | collective-permute-start | bytes 393224 | tf_op jit(solution)/shard_map/ppermute | solution.py:17
  546.8 9.5 %collective-permute-start.12 = (f32[16,2048]{1,0:T(8,128)S(1)}, f32[16,2048]{1,0:T(8,128)S(1)}, u32[]{:S(2)}, u32[]{:S(2)}) collective-permute-start(f32[16,2048]{1,0:T(8,128)S(1)} %fusion.35), channel_id=1, source_target_pairs={{0,8},{8,0},{16,24},{24,16},{32,40},{40,32},{48,56},{56,48},{64,72... | collective-permute-start | bytes 393224 | tf_op jit(solution)/shard_map/ppermute | solution.py:17
  549.0 9.4 %collective-permute-start.1 = (f32[16,2048]{1,0:T(8,128)S(1)}, f32[16,2048]{1,0:T(8,128)S(1)}, u32[]{:S(2)}, u32[]{:S(2)}) collective-permute-start(f32[16,2048]{1,0:T(8,128)S(1)} %add.720), channel_id=1, source_target_pairs={{0,16},{8,24},{16,0},{24,8},{32,48},{40,56},{48,32},{56,40},{64,80... | collective-permute-start | bytes 393224 | tf_op jit(solution)/shard_map/ppermute | solution.py:17
  552.1 8.0 collective-permute-start.5
  554.1 6.2 collective-permute-start.9
  556.3 6.1 collective-permute-start.13
  558.4 6.0 collective-permute-start.2
  560.1 7.5 collective-permute-start.6
  560.9 8.5 collective-permute-start.10
  563.0 9.7 %collective-permute-start.14 = (f32[16,2048]{1,0:T(8,128)}, f32[16,2048]{1,0:T(8,128)}, u32[]{:S(2)}, u32[]{:S(2)}) collective-permute-start(f32[16,2048]{1,0:T(8,128)} %add.779), channel_id=1, source_target_pairs={{0,32},{8,40},{16,48},{24,56},{32,0},{40,8},{48,16},{56,24},{64,96... | collective-permute-start | bytes 393224 | tf_op jit(solution)/shard_map/ppermute | solution.py:17
  565.4 11.7 %collective-permute-start.3 = (f32[16,2048]{1,0:T(8,128)S(1)}, f32[16,2048]{1,0:T(8,128)}, u32[]{:S(2)}, u32[]{:S(2)}) collective-permute-start(f32[16,2048]{1,0:T(8,128)S(1)} %add.722), channel_id=1, source_target_pairs={{0,64},{8,72},{16,80},{24,88},{32,96},{40,104},{48,112},{56,120},{... | collective-permute-start | bytes 393224 | tf_op jit(solution)/shard_map/ppermute | solution.py:17
  568.6 8.5 collective-permute-start.7
  570.4 6.6 collective-permute-start.11
  574.4 5.6 collective-permute-start.15
  (84 other events, 3003.4 us)
Sparse Core Ops, SparseCore 0:
  53.1 78.2 all-gather.4
  133.6 70.4 all-gather.6
  206.2 71.4 all-gather.8
  279.7 71.8 all-gather.10
  759.2 152.4 all-reduce.10
